TPU v7x, 256 devices: a whole 4x4x8 slice. The times are simulated.
256 devices in a mesh: slab: 128 (over y, x, z_hi, core), grp: 2 (over z_lo).
Axes of the slice: x: 4, y: 4, z: 8 (z_hi: 4, z_lo: 2; z = z_hi * 2 + z_lo), core: 2. Of those that a mesh axis runs over, the one named last changes fastest.
Arguments:
- saturation: float32 [256, 64, 256], P(('slab', 'grp')), may hold values from 0.5 to 3
- inlet_mask: int32 [256, 64, 256], P(('slab', 'grp')), may hold values 0 or 1
- crystal_size: float32 [1048576], P(('slab', 'grp')), may hold values from 0.5 to 2
- crystal_weight: float32 [1048576], P(('slab', 'grp')), may hold values from 0.3 to 3
- crystal_cell: int32 [1048576], P(('slab', 'grp')), may hold values from 0 to 32767
- live_count: int32 [256], P(('slab', 'grp')), may hold values from 1024 to 4096, as said below
- nucleus_cell: int32 [256, 4, 512], P(('slab', 'grp')), may hold values from 0 to 32767
- nucleus_count: int32 [256, 4, 512], P(('slab', 'grp')), may hold values from 1 to 8
- migrant_rows: int32 [256, 2, 512], P(('slab', 'grp')), may hold values from 0 to 4095, as said below
- migrant_count: int32 [256, 2], P(('slab', 'grp')), may hold values from 0 to 512
Outputs:
- saturation_out: float32 [256, 64, 256], P(('slab', 'grp'))
- size_out: float32 [1048576], P(('slab', 'grp'))
- arrivals: float32 [256, 2, 2, 512], P(('slab', 'grp'))
Inputs may be any that keep to these rules, and one draw needn't show every extreme that they name: `live_count`: about a quarter of the devices hold exactly 4096 live rows, the others a quarter to a third of that. `migrant_rows`: rows of the device's own parcels below its live count, all distinct; the list toward the lower slab lies in the lower half of the live rows, the other in the upper half.
All inputs are finite; a program needn't handle non-finite values. No bound on the sum of `inlet_mask` on one device may be relied on, other than what follows from the above.
Results may differ from a plain program's by a relative error of at most 0.00007.
Values sent between devices are 32-bit elements; how exact they have to be, the bound alone decides.
A program may use at most 64 MiB of HBM per device.

v0:
```python
import jax
import jax.numpy as jnp
from jax import lax
from jax.sharding import PartitionSpec as P

BLOCK = 2048
STEPS = 2
SUBS = 2
GROWTH = 0.08
VOLUME = 1.0
NUCLEATE = 0.02
DIFFUSE = 0.12
INLET = 4.0


def extended(cells, sides, width):
    for axis, dim in sides:
        count = lax.axis_size(axis)
        ends = count - 1
        head = lax.slice_in_dim(cells, 0, width, axis=dim)
        tail = lax.slice_in_dim(cells, cells.shape[dim] - width, cells.shape[dim], axis=dim)
        cells = jnp.concatenate(
            [
                lax.ppermute(tail, axis, [(i, (i + 1) % count) for i in range(ends)]),
                cells,
                lax.ppermute(head, axis, [((i + 1) % count, i) for i in range(ends)]),
            ],
            axis=dim,
        )
    return cells


def passed_along(value, axis, steps):
    count = lax.axis_size(axis)
    leading, last = (max(0, -steps), min(count, count - steps))
    return lax.ppermute(value, axis, [(source, source + steps) for source in range(leading, last)])


def transport(padded_x, inlet_weight):
    field_mid = padded_x[1:-1]
    padded_yz = jnp.pad(field_mid, ((0, 0), (1, 1), (1, 1)))
    beside = padded_x[2:] + padded_x[:-2]
    beside = beside + padded_yz[:, 2:, 1:-1] + padded_yz[:, :-2, 1:-1]
    beside = beside + padded_yz[:, 1:-1, 2:] + padded_yz[:, 1:-1, :-2]
    field_mid = field_mid + DIFFUSE * (beside - 6.0 * field_mid)
    return field_mid + inlet_weight * (INLET - field_mid)


def cell_tables(cells, line_count, line_width):
    line_of = cells // line_width
    place_of = cells % line_width
    hot_line = (line_of[:, None] == lax.iota(jnp.int32, line_count)[None, :]).astype(jnp.float32)
    hot_place = (place_of[:, None] == lax.iota(jnp.int32, line_width)[None, :]).astype(jnp.float32)
    return (hot_line, hot_place)


def read_cells(slab_lines, hot_line, hot_place):
    picked = jnp.dot(
        hot_line, slab_lines, precision=lax.Precision.HIGHEST, preferred_element_type=jnp.float32
    )
    return jnp.sum(picked * hot_place, axis=1)


def spread_cells(hot_line, hot_place, mass):
    return lax.dot_general(
        hot_line,
        hot_place * mass[:, None],
        (((0,), (0,)), ((), ())),
        precision=lax.Precision.HIGHEST,
        preferred_element_type=jnp.float32,
    )


def parcel_step(
    slab_lines, crystal, crystal_weight, crystal_cell, live_total, event_cell, event_count
):
    line_count, line_width = slab_lines.shape
    parcels = crystal.shape[0]
    event_line, event_place = cell_tables(event_cell, line_count, line_width)
    event_mass = (
        event_count.astype(jnp.float32)
        * NUCLEATE
        * jax.nn.softplus(read_cells(slab_lines, event_line, event_place) - 1.0)
    )
    deposit = spread_cells(event_line, event_place, event_mass)

    def one_block(block_index, state_pair):
        sizes_now, deposit_now = state_pair
        first_row = block_index * BLOCK
        part_size = lax.dynamic_slice_in_dim(sizes_now, first_row, BLOCK)
        part_weight = lax.dynamic_slice_in_dim(crystal_weight, first_row, BLOCK)
        part_cell = lax.dynamic_slice_in_dim(crystal_cell, first_row, BLOCK)
        part_live = (first_row + lax.iota(jnp.int32, BLOCK) < live_total).astype(jnp.float32)
        hot_line, hot_place = cell_tables(part_cell, line_count, line_width)
        local_sat = read_cells(slab_lines, hot_line, hot_place)
        enlarged = part_size + part_live * GROWTH * jax.nn.softplus(local_sat - 1.0)
        consumed = (
            part_live
            * part_weight
            * VOLUME
            * (enlarged * enlarged * enlarged - part_size * part_size * part_size)
        )
        sizes_now = lax.dynamic_update_slice_in_dim(sizes_now, enlarged, first_row, 0)
        return (sizes_now, deposit_now + spread_cells(hot_line, hot_place, consumed))

    block_count = parcels // BLOCK
    crystal, deposit = lax.fori_loop(0, block_count, one_block, (crystal, deposit))
    return (crystal, deposit)


def local(
    saturation,
    inlet_mask,
    crystal_size,
    crystal_weight,
    crystal_cell,
    live_count,
    nucleus_cell,
    nucleus_count,
    migrant_rows,
    migrant_count,
):
    width_z = saturation.shape[2]
    parcels = crystal_size.shape[0]
    slots = migrant_rows.shape[2]
    live_total = live_count[0]
    active_rows = (lax.iota(jnp.int32, parcels) < live_total).astype(jnp.float32)
    inlet_weight = inlet_mask.astype(jnp.float32)
    crystal = crystal_size
    field = saturation
    for step_index in range(STEPS):
        for sub_index in range(SUBS):
            substep = step_index * SUBS + sub_index
            slab_field = lax.all_gather(field, "grp", axis=0, tiled=True)
            crystal, deposit = parcel_step(
                slab_field.reshape(-1, width_z),
                crystal,
                crystal_weight,
                crystal_cell,
                live_total,
                nucleus_cell[0, substep],
                nucleus_count[0, substep],
            )
            field = field - lax.psum_scatter(
                deposit.reshape(slab_field.shape), "grp", scatter_dimension=0, tiled=True
            )
        padded_x = extended(field, ((("slab", "grp"), 0),), 1)
        field = transport(padded_x, inlet_weight)
    size_out = active_rows * crystal
    rows = migrant_rows[0]
    slot_live = (lax.iota(jnp.int32, slots)[None, :] < migrant_count[0][:, None]).astype(
        jnp.float32
    )
    sent = (
        jnp.stack([jnp.take(size_out, rows), jnp.take(crystal_weight, rows)], axis=1)
        * slot_live[:, None, :]
    )
    from_lower = passed_along(sent[1], "slab", 1)
    from_upper = passed_along(sent[0], "slab", -1)
    arrivals = jnp.stack([from_lower, from_upper], axis=0)[None]
    return (field, size_out, arrivals)


def solution(mesh):
    in_specs = (
        P(("slab", "grp"), None, None),
        P(("slab", "grp"), None, None),
        P(("slab", "grp")),
        P(("slab", "grp")),
        P(("slab", "grp")),
        P(("slab", "grp")),
        P(("slab", "grp"), None, None),
        P(("slab", "grp"), None, None),
        P(("slab", "grp"), None, None),
        P(("slab", "grp"), None),
    )
    out_specs = (
        P(("slab", "grp"), None, None),
        P(("slab", "grp")),
        P(("slab", "grp"), None, None, None),
    )
    return jax.shard_map(local, mesh=mesh, in_specs=in_specs, out_specs=out_specs, check_vma=False)
```

profile of v0, /device:TPU:24, one launch (start us, length us, event | category | flops | bytes accessed | tf_op | source)
XLA Modules:
  0.0 174.3 jit_solution(10607794521240898568)
XLA Ops:
  7.2 0.9 convert_multiply_fusion
  8.1 5.1 %all_gather.12 = f32[2,64,256]{2,1,0:T(8,128)S(1)} all-gather(f32[1,64,256]{2,1,0:T(8,128)} %param.20), channel_id=1, replica_groups=mesh['slab'=128,'grp'=2] {'grp'}, dimensions={0}, use_global_device_ids=true | all-gather | bytes 196608 | tf_op jit(solution)/shard_map/all_gather | solution.py:134
  14.6 8.8 %while.68 = (s32[]{:T(128)}, f32[4096]{0:T(1024)S(1)}, f32[128,256]{1,0:T(8,128)S(1)}, s32[]{:T(128)}, s32[4096]{0:T(1024)S(1)}, /*index=5*/f32[128,256]{1,0:T(8...) while((s32[]{:T(128)}, f32[4096]{0:T(1024)S(1)}, ...), condition=%wide.region_3.4_spmd, body=%wide.region_1.3_spmd.sunk | while | flops 1614141440 | bytes 536763 | solution.py:107
  14.6 1.7 fusion.184
  16.3 0.7 fusion.185
  17.3 1.7 fusion.186
  19.1 1.7 fusion.184
  20.7 0.7 fusion.185
  21.7 1.7 fusion.186
  24.2 18.3 %reduce-scatter.5.cloned.1.call-done = f32[1,64,256]{2,1,0:T(8,128)} async-done(((f32[2,64,256]{2,1,0:T(8,128)}), f32[1,64,256]{2,1,0:T(8,128)}) %reduce-scatter.5.cloned.1.call-update) | async-done | bytes 65552 | tf_op jit(solution)/shard_map/reduce_scatter | solution.py:144
  42.5 0.8 sub.150
  43.3 4.9 %all_gather.13 = f32[2,64,256]{2,1,0:T(8,128)S(1)} all-gather(f32[1,64,256]{2,1,0:T(8,128)S(1)} %sub.150), channel_id=1, replica_groups=mesh['slab'=128,'grp'=2] {'grp'}, dimensions={0}, use_global_device_ids=true | all-gather | bytes 196608 | tf_op jit(solution)/shard_map/all_gather | solution.py:134
  49.3 8.8 %while.69 = (s32[]{:T(128)}, f32[4096]{0:T(1024)S(1)}, f32[128,256]{1,0:T(8,128)S(1)}, s32[]{:T(128)}, s32[4096]{0:T(1024)S(1)}, /*index=5*/f32[128,256]{1,0:T(8...) while((s32[]{:T(128)}, f32[4096]{0:T(1024)S(1)}, ...), condition=%wide.region_8.9_spmd, body=%wide.region_6.8_spmd.sunk | while | flops 1614141440 | bytes 536763 | solution.py:107
  49.4 1.7 fusion.190
  51.0 0.7 fusion.191
  52.1 1.7 fusion.192
  53.8 1.7 fusion.190
  55.5 0.7 fusion.191
  56.5 1.7 fusion.192
  59.0 16.0 %reduce-scatter.7.cloned.1.call-done = f32[1,64,256]{2,1,0:T(8,128)} async-done(((f32[2,64,256]{2,1,0:T(8,128)}), f32[1,64,256]{2,1,0:T(8,128)}) %reduce-scatter.7.cloned.1.call-update) | async-done | bytes 65552 | tf_op jit(solution)/shard_map/reduce_scatter | solution.py:144
  74.9 0.8 sub.153
  75.8 6.7 %collective-permute-start = (f32[1,64,256]{2,1,0:T(8,128)S(1)}, f32[1,64,256]{2,1,0:T(8,128)S(1)}, u32[]{:S(2)}, u32[]{:S(2)}) collective-permute-start(f32[1,64,256]{2,1,0:T(8,128)S(1)} %sub.153), channel_id=1, source_target_pairs={{1,0},{2,1},{3,2},{4,3},{5,4},{6,5},{7,6},{8,7},{9,8},{10,9},{11,1... | collective-permute-start | bytes 196616 | tf_op jit(solution)/shard_map/ppermute | solution.py:26
  82.4 1.9 %collective-permute-start.1 = (f32[1,64,256]{2,1,0:T(8,128)S(1)}, f32[1,64,256]{2,1,0:T(8,128)S(1)}, u32[]{:S(2)}, u32[]{:S(2)}) collective-permute-start(f32[1,64,256]{2,1,0:T(8,128)S(1)} %sub.153), channel_id=1, source_target_pairs={{0,1},{1,2},{2,3},{3,4},{4,5},{5,6},{6,7},{7,8},{8,9},{9,10},{10,1... | collective-permute-start | bytes 196616 | tf_op jit(solution)/shard_map/ppermute | solution.py:24
  84.4 7.8 %collective-permute-done.1 = f32[1,64,256]{2,1,0:T(8,128)S(1)} collective-permute-done((f32[1,64,256]{2,1,0:T(8,128)S(1)}, f32[1,64,256]{2,1,0:T(8,128)S(1)}, u32[]{:S(2)}, u32[]{:S(2)}) %collective-permute-start.1) | collective-permute-done | bytes 65568 | tf_op jit(solution)/shard_map/ppermute | solution.py:24
  92.3 4.9 %all_gather.14 = f32[2,64,256]{2,1,0:T(8,128)S(1)} all-gather(f32[1,64,256]{2,1,0:T(8,128)S(1)} %multiply_add_fusion.1), channel_id=1, replica_groups=mesh['slab'=128,'grp'=2] {'grp'}, dimensions={0}, use_global_device_ids=true | all-gather | bytes 196608 | tf_op jit(solution)/shard_map/all_gather | solution.py:134
  98.3 8.8 %while.70 = (s32[]{:T(128)}, f32[4096]{0:T(1024)S(1)}, f32[128,256]{1,0:T(8,128)S(1)}, s32[]{:T(128)}, s32[4096]{0:T(1024)S(1)}, /*index=5*/f32[128,256]{1,0:T(8...) while((s32[]{:T(128)}, f32[4096]{0:T(1024)S(1)}, ...), condition=%wide.region_13.14_spmd, body=%wide.region_11.13_spmd.sunk | while | flops 1614141440 | bytes 536763 | solution.py:107
  98.4 1.7 fusion.196
  101.1 1.7 fusion.198
  102.8 1.7 fusion.196
  105.5 1.7 fusion.198
  108.7 6.2 %gather_fusion.1 = f32[1024]{0:T(1024)S(1)} fusion(f32[4096]{0:T(1024)S(1)} %get-tuple-element.1170, s32[1024]{0:T(1024)S(1)} %broadcast_clamp_fusion), kind=kCustom, calls=%fused_computation.1.clone | custom fusion | bytes 12288 | tf_op jit(solution)/shard_map/jit(_take)/gather | solution.py:155
  114.8 2.1 %reduce-scatter.9.cloned.1.call-done = f32[1,64,256]{2,1,0:T(8,128)} async-done(((f32[2,64,256]{2,1,0:T(8,128)}), f32[1,64,256]{2,1,0:T(8,128)}) %reduce-scatter.9.cloned.1.call-update) | async-done | bytes 65552 | tf_op jit(solution)/shard_map/reduce_scatter | solution.py:144
  117.0 0.8 sub.158
  117.8 5.1 %all_gather.15 = f32[2,64,256]{2,1,0:T(8,128)S(1)} all-gather(f32[1,64,256]{2,1,0:T(8,128)S(1)} %sub.158), channel_id=1, replica_groups=mesh['slab'=128,'grp'=2] {'grp'}, dimensions={0}, use_global_device_ids=true | all-gather | bytes 196608 | tf_op jit(solution)/shard_map/all_gather | solution.py:134
  124.0 8.8 %while.71 = (s32[]{:T(128)}, f32[4096]{0:T(1024)S(1)}, f32[128,256]{1,0:T(8,128)S(1)}, s32[]{:T(128)}, s32[4096]{0:T(1024)S(1)}, /*index=5*/f32[128,256]{1,0:T(8...) while((s32[]{:T(128)}, f32[4096]{0:T(1024)S(1)}, ...), condition=%wide.region_18.19_spmd, body=%wide.region_16.18_spmd.sunk | while | flops 1614141440 | bytes 536763 | solution.py:107
  124.1 1.7 fusion.202
  126.7 1.7 fusion.204
  128.5 1.7 fusion.202
  131.1 1.7 fusion.204
  133.6 6.2 %gather_fusion = f32[1024]{0:T(1024)S(1)} fusion(f32[4096]{0:T(1024)S(1)} %fusion.130, s32[1024]{0:T(1024)S(1)} %broadcast_clamp_fusion), kind=kCustom, calls=%fused_computation.clone | custom fusion | bytes 12288 | tf_op jit(solution)/shard_map/jit(_take)/gather | solution.py:155
  139.8 5.6 %collective-permute-start.5 = (f32[2,512]{1,0:T(2,128)S(1)}, f32[2,512]{1,0:T(2,128)S(1)}, u32[]{:S(2)}, u32[]{:S(2)}) collective-permute-start(f32[2,512]{1,0:T(2,128)S(1)} %get-tuple-element.809), channel_id=1, source_target_pairs={{2,0},{4,2},{6,4},{8,6},{10,8},{12,10},{14,12},{16,14},{18,16},{20... | collective-permute-start | bytes 12296 | tf_op jit(solution)/shard_map/ppermute | solution.py:36
  145.4 1.9 %collective-permute-start.4 = (f32[2,512]{1,0:T(2,128)S(1)}, f32[2,512]{1,0:T(2,128)S(1)}, u32[]{:S(2)}, u32[]{:S(2)}) collective-permute-start(f32[2,512]{1,0:T(2,128)S(1)} %get-tuple-element.808), channel_id=1, source_target_pairs={{0,2},{2,4},{4,6},{6,8},{8,10},{10,12},{12,14},{14,16},{16,18},{18... | collective-permute-start | bytes 12296 | tf_op jit(solution)/shard_map/ppermute | solution.py:36
  147.3 2.3 %reduce-scatter.11.cloned.1.call-done = f32[1,64,256]{2,1,0:T(8,128)} async-done(((f32[2,64,256]{2,1,0:T(8,128)}), f32[1,64,256]{2,1,0:T(8,128)}) %reduce-scatter.11.cloned.1.call-update) | async-done | bytes 65552 | tf_op jit(solution)/shard_map/reduce_scatter | solution.py:144
  149.6 0.8 sub.161
  150.5 6.7 %collective-permute-start.2 = (f32[1,64,256]{2,1,0:T(8,128)S(1)}, f32[1,64,256]{2,1,0:T(8,128)S(1)}, u32[]{:S(2)}, u32[]{:S(2)}) collective-permute-start(f32[1,64,256]{2,1,0:T(8,128)S(1)} %sub.161), channel_id=1, source_target_pairs={{1,0},{2,1},{3,2},{4,3},{5,4},{6,5},{7,6},{8,7},{9,8},{10,9},{11,1... | collective-permute-start | bytes 196616 | tf_op jit(solution)/shard_map/ppermute | solution.py:26
  157.2 1.9 %collective-permute-start.3 = (f32[1,64,256]{2,1,0:T(8,128)S(1)}, f32[1,64,256]{2,1,0:T(8,128)S(1)}, u32[]{:S(2)}, u32[]{:S(2)}) collective-permute-start(f32[1,64,256]{2,1,0:T(8,128)S(1)} %sub.161), channel_id=1, source_target_pairs={{0,1},{1,2},{2,3},{3,4},{4,5},{5,6},{6,7},{7,8},{8,9},{9,10},{10,1... | collective-permute-start | bytes 196616 | tf_op jit(solution)/shard_map/ppermute | solution.py:24
  159.7 7.2 %collective-permute-done.3 = f32[1,64,256]{2,1,0:T(8,128)S(1)} collective-permute-done((f32[1,64,256]{2,1,0:T(8,128)S(1)}, f32[1,64,256]{2,1,0:T(8,128)S(1)}, u32[]{:S(2)}, u32[]{:S(2)}) %collective-permute-start.3) | collective-permute-done | bytes 65568 | tf_op jit(solution)/shard_map/ppermute | solution.py:24
  167.0 0.7 multiply_add_fusion
  (97 shorter events, 13.6 us)
Async XLA Ops:
  7.2 6.1 %copy-start.11 = (s32[1,4,512]{2,1,0:T(4,128)S(1)}, s32[1,4,512]{2,1,0:T(4,128)}, u32[]{:S(2)}) copy-start(s32[1,4,512]{2,1,0:T(4,128)} %param.26) | copy-start | bytes 24580
  7.2 35.3 %reduce-scatter.5.cloned.1.call-start = ((), (), s32[]{:S(2)}) async-start(), calls=%async_computation.4 | async-start | bytes 196608 | tf_op jit(solution)/shard_map/reduce_scatter | solution.py:144
  13.8 0.7 copy-start
  13.8 0.7 copy-start.2
  13.8 0.7 copy-start.3
  23.4 0.7 copy-start.9
  23.4 19.1 %copy-start.4 = (f32[1,64,256]{2,1,0:T(8,128)S(1)}, f32[1,64,256]{2,1,0:T(8,128)}, u32[]{:S(2)}) copy-start(f32[1,64,256]{2,1,0:T(8,128)} %param.20) | copy-start | bytes 196612
  24.1 50.8 %reduce-scatter.7.cloned.1.call-start = ((), (), s32[]{:S(2)}) async-start(), calls=%async_computation.5 | async-start | bytes 196608 | tf_op jit(solution)/shard_map/reduce_scatter | solution.py:144
  58.2 0.7 copy-start.6
  58.2 0.7 copy-start.10
  58.9 33.4 %copy-start.5 = (s32[1,64,256]{2,1,0:T(8,128)S(1)}, s32[1,64,256]{2,1,0:T(8,128)}, u32[]{:S(2)}) copy-start(s32[1,64,256]{2,1,0:T(8,128)} %param.21) | copy-start | bytes 196612
  58.9 58.1 %reduce-scatter.9.cloned.1.call-start = ((), (), s32[]{:S(2)}) async-start(), calls=%async_computation.6 | async-start | bytes 196608 | tf_op jit(solution)/shard_map/reduce_scatter | solution.py:144
  75.8 8.6 %collective-permute-start = (f32[1,64,256]{2,1,0:T(8,128)S(1)}, f32[1,64,256]{2,1,0:T(8,128)S(1)}, u32[]{:S(2)}, u32[]{:S(2)}) collective-permute-start(f32[1,64,256]{2,1,0:T(8,128)S(1)} %sub.153), channel_id=1, source_target_pairs={{1,0},{2,1},{3,2},{4,3},{5,4},{6,5},{7,6},{8,7},{9,8},{10,9},{11,1... | collective-permute-start | bytes 196616 | tf_op jit(solution)/shard_map/ppermute | solution.py:26
  82.4 9.8 %collective-permute-start.1 = (f32[1,64,256]{2,1,0:T(8,128)S(1)}, f32[1,64,256]{2,1,0:T(8,128)S(1)}, u32[]{:S(2)}, u32[]{:S(2)}) collective-permute-start(f32[1,64,256]{2,1,0:T(8,128)S(1)} %sub.153), channel_id=1, source_target_pairs={{0,1},{1,2},{2,3},{3,4},{4,5},{5,6},{6,7},{7,8},{8,9},{9,10},{10,1... | collective-permute-start | bytes 196616 | tf_op jit(solution)/shard_map/ppermute | solution.py:24
  107.2 0.7 copy-start.7
  107.2 0.7 copy-start.12
  107.9 41.8 %reduce-scatter.11.cloned.1.call-start = ((), (), s32[]{:S(2)}) async-start(), calls=%async_computation.7 | async-start | bytes 196608 | tf_op jit(solution)/shard_map/reduce_scatter | solution.py:144
  132.9 0.7 copy-start.8
  133.6 6.2 %copy-start.1 = (f32[4096]{0:T(1024)}, f32[4096]{0:T(1024)S(1)}, u32[]{:S(2)}) copy-start(f32[4096]{0:T(1024)S(1)} %fusion.130) | copy-start | bytes 49156
  139.8 19.3 %collective-permute-start.5 = (f32[2,512]{1,0:T(2,128)S(1)}, f32[2,512]{1,0:T(2,128)S(1)}, u32[]{:S(2)}, u32[]{:S(2)}) collective-permute-start(f32[2,512]{1,0:T(2,128)S(1)} %get-tuple-element.809), channel_id=1, source_target_pairs={{2,0},{4,2},{6,4},{8,6},{10,8},{12,10},{14,12},{16,14},{18,16},{20... | collective-permute-start | bytes 12296 | tf_op jit(solution)/shard_map/ppermute | solution.py:36
  145.4 13.7 %collective-permute-start.4 = (f32[2,512]{1,0:T(2,128)S(1)}, f32[2,512]{1,0:T(2,128)S(1)}, u32[]{:S(2)}, u32[]{:S(2)}) collective-permute-start(f32[2,512]{1,0:T(2,128)S(1)} %get-tuple-element.808), channel_id=1, source_target_pairs={{0,2},{2,4},{4,6},{6,8},{8,10},{10,12},{12,14},{14,16},{16,18},{18... | collective-permute-start | bytes 12296 | tf_op jit(solution)/shard_map/ppermute | solution.py:36
  150.5 9.3 %collective-permute-start.2 = (f32[1,64,256]{2,1,0:T(8,128)S(1)}, f32[1,64,256]{2,1,0:T(8,128)S(1)}, u32[]{:S(2)}, u32[]{:S(2)}) collective-permute-start(f32[1,64,256]{2,1,0:T(8,128)S(1)} %sub.161), channel_id=1, source_target_pairs={{1,0},{2,1},{3,2},{4,3},{5,4},{6,5},{7,6},{8,7},{9,8},{10,9},{11,1... | collective-permute-start | bytes 196616 | tf_op jit(solution)/shard_map/ppermute | solution.py:26
  157.2 9.8 %collective-permute-start.3 = (f32[1,64,256]{2,1,0:T(8,128)S(1)}, f32[1,64,256]{2,1,0:T(8,128)S(1)}, u32[]{:S(2)}, u32[]{:S(2)}) collective-permute-start(f32[1,64,256]{2,1,0:T(8,128)S(1)} %sub.161), channel_id=1, source_target_pairs={{0,1},{1,2},{2,3},{3,4},{4,5},{5,6},{6,7},{7,8},{8,9},{9,10},{10,1... | collective-permute-start | bytes 196616 | tf_op jit(solution)/shard_map/ppermute | solution.py:24
Sparse Core Ops, SparseCore 0:
  24.2 18.2 reduce-scatter.4
  59.0 15.8 reduce-scatter.6
  108.0 8.9 reduce-scatter.8
  133.7 15.9 reduce-scatter.10
where the time goes:
time: 175 us; the launch traced here: 174 us
  waiting for transfers between devices  53.9 us (31%)
  matrix products  30.9 us (18%)
  starting transfers between devices  24.9 us (14%)
  blocking collectives  20.1 us (11%)
  local copies, waits for them, and re-layouts  17.7 us (10%)
  between operations  14.9 us (9%)
  other arithmetic  11.5 us (7%)
    reduce_scatter x4, waiting for transfers between devices, local(): lax.psum_scatter(deposit.reshape(slab_field.shape), 'grp', scatter_dimens...  38.7 us
    all_gather x4, blocking collectives, local(): slab_field = lax.all_gather(field, 'grp', axis=0, tiled=True)  20.1 us
    dot_general x12, matrix products, spread_cells(): lax.dot_general(hot_line, hot_place * mass[:, None], (((0,), (0,)), ((),...  15.5 us
    dot_general x12, matrix products, read_cells(): jnp.dot(hot_line, slab_lines, precision=lax.Precision.HIGHEST, preferred_...  15.4 us
    ppermute x2, waiting for transfers between devices, extended(): lax.ppermute(tail, axis, [(i, (i + 1) % count) for i in range(ends)])  15.1 us
    ppermute x2, starting transfers between devices, extended(): lax.ppermute(head, axis, [((i + 1) % count, i) for i in range(ends)])  13.3 us
    ppermute x2, starting transfers between devices, passed_along(): lax.ppermute(value, axis, [(source, source + steps) for source in range(l...  7.5 us
    gather x2, local copies, waits for them, and re-layouts, local(): jnp.take(crystal_weight, rows)  6.16 us
  transfers between devices with their start and end apart: 10, of which 6 were waited for; matrix products, arithmetic and copies ran while one was open for 8% of the time, Pallas kernels for 0%

commit v1 on v0

--- a/solution.py
+++ b/solution.py
@@ -131,7 +131,9 @@
     for step_index in range(STEPS):
         for sub_index in range(SUBS):
             substep = step_index * SUBS + sub_index
-            slab_field = lax.all_gather(field, "grp", axis=0, tiled=True)
+            slab_field = jnp.concatenate(
+                lax.all_to_all(jnp.stack([field] * lax.axis_size("grp")), "grp", 0, 0), axis=0
+            )
             crystal, deposit = parcel_step(
                 slab_field.reshape(-1, width_z),
                 crystal,

time: 175 us -> 189 us (1.080)
  blocking collectives: 20.1 us -> 0 us
  waiting for transfers between devices: 53.9 us -> 71.4 us
  starting transfers between devices: 24.9 us -> 38.7 us
  other arithmetic: 11.5 us -> 14.2 us
    all_gather x4 -> x0, blocking collectives: 20.1 us -> none  [local(): slab_field = lax.all_gather(field, 'grp', axis=0, tiled=True)]
    all_to_all x0 -> x4, waiting for transfers between devices: none -> 17.3 us  [local(): lax.all_to_all(jnp.stack([field] * lax.axis_size('grp')), 'grp', 0, 0)]
    all_to_all x0 -> x4, starting transfers between devices: none -> 13.8 us  [local(): lax.all_to_all(jnp.stack([field] * lax.axis_size('grp')), 'grp', 0, 0)]
    another operation x0 -> x4, other arithmetic: none -> 3.52 us  [local(): jnp.stack([field] * lax.axis_size('grp'))]
  transfers between devices with their start and end apart: 10 -> 14, of which waited for: 6 -> 10; matrix products, arithmetic and copies ran while one was open for 8% -> 7% of each run, Pallas kernels for 0% -> 0%
where the time goes in v1:
time: 189 us; the launch traced here: 188 us
  waiting for transfers between devices  71.4 us (38%)
  starting transfers between devices  38.7 us (20%)
  matrix products  30.9 us (16%)
  local copies, waits for them, and re-layouts  17.6 us (9%)
  between operations  14.9 us (8%)
  other arithmetic  14.2 us (8%)
    reduce_scatter x4, waiting for transfers between devices, local(): lax.psum_scatter(deposit.reshape(slab_field.shape), 'grp', scatter_dimens...  39 us
    all_to_all x4, waiting for transfers between devices, local(): lax.all_to_all(jnp.stack([field] * lax.axis_size('grp')), 'grp', 0, 0)  17.3 us
    dot_general x12, matrix products, spread_cells(): lax.dot_general(hot_line, hot_place * mass[:, None], (((0,), (0,)), ((),...  15.5 us
    dot_general x12, matrix products, read_cells(): jnp.dot(hot_line, slab_lines, precision=lax.Precision.HIGHEST, preferred_...  15.4 us
    ppermute x2, waiting for transfers between devices, extended(): lax.ppermute(tail, axis, [(i, (i + 1) % count) for i in range(ends)])  15.1 us
    all_to_all x4, starting transfers between devices, local(): lax.all_to_all(jnp.stack([field] * lax.axis_size('grp')), 'grp', 0, 0)  13.8 us
    ppermute x2, starting transfers between devices, extended(): lax.ppermute(head, axis, [((i + 1) % count, i) for i in range(ends)])  13.3 us
    ppermute x2, starting transfers between devices, passed_along(): lax.ppermute(value, axis, [(source, source + steps) for source in range(l...  7.5 us
  transfers between devices with their start and end apart: 14, of which 10 were waited for; matrix products, arithmetic and copies ran while one was open for 7% of the time, Pallas kernels for 0%

profile of v1, /device:TPU:24, one launch (start us, length us, event | category | flops | bytes accessed | tf_op | source)
XLA Modules:
  0.0 188.2 jit_solution(1140903395453480010)
XLA Ops:
  7.2 1.6 pad_maximum_fusion
  8.7 3.5 %all-to-all-start = ((f32[2,1,64,256]{3,2,1,0:T(8,128)}), f32[2,1,64,256]{3,2,1,0:T(8,128)S(1)}, u32[]{:S(2)}, u32[]{:S(2)}) async-start(f32[2,1,64,256]{3,2,1,0:T(8,128)} %pad_maximum_fusion), calls=%async_computation | async-start | bytes 262144 | tf_op jit(solution)/shard_map/all_to_all | solution.py:135
  12.4 4.3 %all-to-all-done = f32[2,1,64,256]{3,2,1,0:T(8,128)S(1)} async-done(((f32[2,1,64,256]{3,2,1,0:T(8,128)}), f32[2,1,64,256]{3,2,1,0:T(8,128)S(1)}, u32[]{:S(2)}, u32[]{:S(2)}) %all-to-all-start) | async-done | bytes 131104 | tf_op jit(solution)/shard_map/all_to_all | solution.py:135
  18.0 8.8 %while.68 = (s32[]{:T(128)}, f32[4096]{0:T(1024)S(1)}, f32[128,256]{1,0:T(8,128)S(1)}, s32[]{:T(128)}, s32[4096]{0:T(1024)S(1)}, /*index=5*/f32[128,256]{1,0:T(8...) while((s32[]{:T(128)}, f32[4096]{0:T(1024)S(1)}, ...), condition=%wide.region_3.4_spmd, body=%wide.region_1.3_spmd.sunk | while | flops 1614141440 | bytes 536763 | solution.py:107
  18.1 1.7 fusion.184
  20.7 1.7 fusion.186
  22.5 1.7 fusion.184
  25.1 1.7 fusion.186
  27.5 18.4 %reduce-scatter.5.cloned.1.call-done = f32[1,64,256]{2,1,0:T(8,128)} async-done(((f32[2,64,256]{2,1,0:T(8,128)}), f32[1,64,256]{2,1,0:T(8,128)}) %reduce-scatter.5.cloned.1.call-update) | async-done | bytes 65552 | tf_op jit(solution)/shard_map/reduce_scatter | solution.py:146
  45.9 0.8 sub.150
  47.4 3.4 %all-to-all-start.1 = ((f32[2,1,64,256]{3,2,1,0:T(8,128)}), f32[2,1,64,256]{3,2,1,0:T(8,128)S(1)}, u32[]{:S(2)}, u32[]{:S(2)}) async-start(f32[2,1,64,256]{3,2,1,0:T(8,128)} %pad_maximum_fusion.1), calls=%async_computation.2 | async-start | bytes 262144 | tf_op jit(solution)/shard_map/all_to_all | solution.py:135
  50.9 4.4 %all-to-all-done.1 = f32[2,1,64,256]{3,2,1,0:T(8,128)S(1)} async-done(((f32[2,1,64,256]{3,2,1,0:T(8,128)}), f32[2,1,64,256]{3,2,1,0:T(8,128)S(1)}, u32[]{:S(2)}, u32[]{:S(2)}) %all-to-all-start.1) | async-done | bytes 131104 | tf_op jit(solution)/shard_map/all_to_all | solution.py:135
  56.3 8.8 %while.69 = (s32[]{:T(128)}, f32[4096]{0:T(1024)S(1)}, f32[128,256]{1,0:T(8,128)S(1)}, s32[]{:T(128)}, s32[4096]{0:T(1024)S(1)}, /*index=5*/f32[128,256]{1,0:T(8...) while((s32[]{:T(128)}, f32[4096]{0:T(1024)S(1)}, ...), condition=%wide.region_8.9_spmd, body=%wide.region_6.8_spmd.sunk | while | flops 1614141440 | bytes 536763 | solution.py:107
  56.4 1.7 fusion.190
  59.0 1.7 fusion.192
  60.8 1.7 fusion.190
  63.4 1.7 fusion.192
  65.8 16.0 %reduce-scatter.7.cloned.1.call-done = f32[1,64,256]{2,1,0:T(8,128)} async-done(((f32[2,64,256]{2,1,0:T(8,128)}), f32[1,64,256]{2,1,0:T(8,128)}) %reduce-scatter.7.cloned.1.call-update) | async-done | bytes 65552 | tf_op jit(solution)/shard_map/reduce_scatter | solution.py:146
  81.9 0.8 sub.153
  82.7 6.6 %collective-permute-start = (f32[1,64,256]{2,1,0:T(8,128)S(1)}, f32[1,64,256]{2,1,0:T(8,128)S(1)}, u32[]{:S(2)}, u32[]{:S(2)}) collective-permute-start(f32[1,64,256]{2,1,0:T(8,128)S(1)} %sub.153), channel_id=1, source_target_pairs={{1,0},{2,1},{3,2},{4,3},{5,4},{6,5},{7,6},{8,7},{9,8},{10,9},{11,1... | collective-permute-start | bytes 196616 | tf_op jit(solution)/shard_map/ppermute | solution.py:26
  89.4 1.9 %collective-permute-start.1 = (f32[1,64,256]{2,1,0:T(8,128)S(1)}, f32[1,64,256]{2,1,0:T(8,128)S(1)}, u32[]{:S(2)}, u32[]{:S(2)}) collective-permute-start(f32[1,64,256]{2,1,0:T(8,128)S(1)} %sub.153), channel_id=1, source_target_pairs={{0,1},{1,2},{2,3},{3,4},{4,5},{5,6},{6,7},{7,8},{8,9},{9,10},{10,1... | collective-permute-start | bytes 196616 | tf_op jit(solution)/shard_map/ppermute | solution.py:24
  91.4 7.8 %collective-permute-done.1 = f32[1,64,256]{2,1,0:T(8,128)S(1)} collective-permute-done((f32[1,64,256]{2,1,0:T(8,128)S(1)}, f32[1,64,256]{2,1,0:T(8,128)S(1)}, u32[]{:S(2)}, u32[]{:S(2)}) %collective-permute-start.1) | collective-permute-done | bytes 65568 | tf_op jit(solution)/shard_map/ppermute | solution.py:24
  100.0 3.4 %all-to-all-start.2 = ((f32[2,1,64,256]{3,2,1,0:T(8,128)}), f32[2,1,64,256]{3,2,1,0:T(8,128)S(1)}, u32[]{:S(2)}, u32[]{:S(2)}) async-start(f32[2,1,64,256]{3,2,1,0:T(8,128)} %pad_maximum_fusion.2), calls=%async_computation.4 | async-start | bytes 262144 | tf_op jit(solution)/shard_map/all_to_all | solution.py:135
  103.4 4.4 %all-to-all-done.2 = f32[2,1,64,256]{3,2,1,0:T(8,128)S(1)} async-done(((f32[2,1,64,256]{3,2,1,0:T(8,128)}), f32[2,1,64,256]{3,2,1,0:T(8,128)S(1)}, u32[]{:S(2)}, u32[]{:S(2)}) %all-to-all-start.2) | async-done | bytes 131104 | tf_op jit(solution)/shard_map/all_to_all | solution.py:135
  108.8 8.8 %while.70 = (s32[]{:T(128)}, f32[4096]{0:T(1024)S(1)}, f32[128,256]{1,0:T(8,128)S(1)}, s32[]{:T(128)}, s32[4096]{0:T(1024)S(1)}, /*index=5*/f32[128,256]{1,0:T(8...) while((s32[]{:T(128)}, f32[4096]{0:T(1024)S(1)}, ...), condition=%wide.region_13.14_spmd, body=%wide.region_11.13_spmd.sunk | while | flops 1614141440 | bytes 536763 | solution.py:107
  108.9 1.7 fusion.196
  111.6 1.7 fusion.198
  113.4 1.7 fusion.196
  116.0 1.7 fusion.198
  119.0 6.2 %gather_fusion.1 = f32[1024]{0:T(1024)S(1)} fusion(f32[4096]{0:T(1024)S(1)} %get-tuple-element.1170, s32[1024]{0:T(1024)S(1)} %broadcast_clamp_fusion), kind=kCustom, calls=%fused_computation.1.clone | custom fusion | bytes 12288 | tf_op jit(solution)/shard_map/jit(_take)/gather | solution.py:157
  125.2 2.3 %reduce-scatter.9.cloned.1.call-done = f32[1,64,256]{2,1,0:T(8,128)} async-done(((f32[2,64,256]{2,1,0:T(8,128)}), f32[1,64,256]{2,1,0:T(8,128)}) %reduce-scatter.9.cloned.1.call-update) | async-done | bytes 65552 | tf_op jit(solution)/shard_map/reduce_scatter | solution.py:146
  127.5 0.8 sub.158
  129.0 3.5 %all-to-all-start.3 = ((f32[2,1,64,256]{3,2,1,0:T(8,128)}), f32[2,1,64,256]{3,2,1,0:T(8,128)S(1)}, u32[]{:S(2)}, u32[]{:S(2)}) async-start(f32[2,1,64,256]{3,2,1,0:T(8,128)} %pad_maximum_fusion.3), calls=%async_computation.6 | async-start | bytes 262144 | tf_op jit(solution)/shard_map/all_to_all | solution.py:135
  132.8 4.1 %all-to-all-done.3 = f32[2,1,64,256]{3,2,1,0:T(8,128)S(1)} async-done(((f32[2,1,64,256]{3,2,1,0:T(8,128)}), f32[2,1,64,256]{3,2,1,0:T(8,128)S(1)}, u32[]{:S(2)}, u32[]{:S(2)}) %all-to-all-start.3) | async-done | bytes 131104 | tf_op jit(solution)/shard_map/all_to_all | solution.py:135
  138.0 8.8 %while.71 = (s32[]{:T(128)}, f32[4096]{0:T(1024)S(1)}, f32[128,256]{1,0:T(8,128)S(1)}, s32[]{:T(128)}, s32[4096]{0:T(1024)S(1)}, /*index=5*/f32[128,256]{1,0:T(8...) while((s32[]{:T(128)}, f32[4096]{0:T(1024)S(1)}, ...), condition=%wide.region_18.19_spmd, body=%wide.region_16.18_spmd.sunk | while | flops 1614141440 | bytes 536763 | solution.py:107
  138.1 1.7 fusion.202
  140.7 1.7 fusion.204
  142.5 1.7 fusion.202
  145.2 1.7 fusion.204
  147.6 6.2 %gather_fusion = f32[1024]{0:T(1024)S(1)} fusion(f32[4096]{0:T(1024)S(1)} %fusion.130, s32[1024]{0:T(1024)S(1)} %broadcast_clamp_fusion), kind=kCustom, calls=%fused_computation.clone | custom fusion | bytes 12288 | tf_op jit(solution)/shard_map/jit(_take)/gather | solution.py:157
  153.8 5.6 %collective-permute-start.5 = (f32[2,512]{1,0:T(2,128)S(1)}, f32[2,512]{1,0:T(2,128)S(1)}, u32[]{:S(2)}, u32[]{:S(2)}) collective-permute-start(f32[2,512]{1,0:T(2,128)S(1)} %get-tuple-element.809), channel_id=1, source_target_pairs={{2,0},{4,2},{6,4},{8,6},{10,8},{12,10},{14,12},{16,14},{18,16},{20... | collective-permute-start | bytes 12296 | tf_op jit(solution)/shard_map/ppermute | solution.py:36
  159.4 1.9 %collective-permute-start.4 = (f32[2,512]{1,0:T(2,128)S(1)}, f32[2,512]{1,0:T(2,128)S(1)}, u32[]{:S(2)}, u32[]{:S(2)}) collective-permute-start(f32[2,512]{1,0:T(2,128)S(1)} %get-tuple-element.808), channel_id=1, source_target_pairs={{0,2},{2,4},{4,6},{6,8},{8,10},{10,12},{12,14},{14,16},{16,18},{18... | collective-permute-start | bytes 12296 | tf_op jit(solution)/shard_map/ppermute | solution.py:36
  161.3 2.3 %reduce-scatter.11.cloned.1.call-done = f32[1,64,256]{2,1,0:T(8,128)} async-done(((f32[2,64,256]{2,1,0:T(8,128)}), f32[1,64,256]{2,1,0:T(8,128)}) %reduce-scatter.11.cloned.1.call-update) | async-done | bytes 65552 | tf_op jit(solution)/shard_map/reduce_scatter | solution.py:146
  163.6 0.8 sub.161
  164.5 6.6 %collective-permute-start.2 = (f32[1,64,256]{2,1,0:T(8,128)S(1)}, f32[1,64,256]{2,1,0:T(8,128)S(1)}, u32[]{:S(2)}, u32[]{:S(2)}) collective-permute-start(f32[1,64,256]{2,1,0:T(8,128)S(1)} %sub.161), channel_id=1, source_target_pairs={{1,0},{2,1},{3,2},{4,3},{5,4},{6,5},{7,6},{8,7},{9,8},{10,9},{11,1... | collective-permute-start | bytes 196616 | tf_op jit(solution)/shard_map/ppermute | solution.py:26
  171.1 1.9 %collective-permute-start.3 = (f32[1,64,256]{2,1,0:T(8,128)S(1)}, f32[1,64,256]{2,1,0:T(8,128)S(1)}, u32[]{:S(2)}, u32[]{:S(2)}) collective-permute-start(f32[1,64,256]{2,1,0:T(8,128)S(1)} %sub.161), channel_id=1, source_target_pairs={{0,1},{1,2},{2,3},{3,4},{4,5},{5,6},{6,7},{7,8},{8,9},{9,10},{10,1... | collective-permute-start | bytes 196616 | tf_op jit(solution)/shard_map/ppermute | solution.py:24
  173.7 7.2 %collective-permute-done.3 = f32[1,64,256]{2,1,0:T(8,128)S(1)} collective-permute-done((f32[1,64,256]{2,1,0:T(8,128)S(1)}, f32[1,64,256]{2,1,0:T(8,128)S(1)}, u32[]{:S(2)}, u32[]{:S(2)}) %collective-permute-start.3) | collective-permute-done | bytes 65568 | tf_op jit(solution)/shard_map/ppermute | solution.py:24
  180.9 0.7 multiply_add_fusion
  (107 shorter events, 18.4 us)
Async XLA Ops:
  8.7 3.6 %copy-start.11 = (s32[1,4,512]{2,1,0:T(4,128)S(1)}, s32[1,4,512]{2,1,0:T(4,128)}, u32[]{:S(2)}) copy-start(s32[1,4,512]{2,1,0:T(4,128)} %param.27) | copy-start | bytes 24580
  8.7 3.6 %copy-start.12 = (s32[1,4,512]{2,1,0:T(4,128)S(1)}, s32[1,4,512]{2,1,0:T(4,128)}, u32[]{:S(2)}) copy-start(s32[1,4,512]{2,1,0:T(4,128)} %param.26) | copy-start | bytes 24580
  8.7 8.0 %all-to-all-start = ((f32[2,1,64,256]{3,2,1,0:T(8,128)}), f32[2,1,64,256]{3,2,1,0:T(8,128)S(1)}, u32[]{:S(2)}, u32[]{:S(2)}) async-start(f32[2,1,64,256]{3,2,1,0:T(8,128)} %pad_maximum_fusion), calls=%async_computation | async-start | bytes 262144 | tf_op jit(solution)/shard_map/all_to_all | solution.py:135
  12.2 33.7 %reduce-scatter.5.cloned.1.call-start = ((), (), s32[]{:S(2)}) async-start(), calls=%async_computation.8 | async-start | bytes 196608 | tf_op jit(solution)/shard_map/reduce_scatter | solution.py:146
  17.3 0.7 copy-start
  17.3 0.7 copy-start.2
  17.3 0.7 copy-start.3
  26.8 0.6 copy-start.9
  26.9 19.0 %copy-start.4 = (f32[1,64,256]{2,1,0:T(8,128)S(1)}, f32[1,64,256]{2,1,0:T(8,128)}, u32[]{:S(2)}) copy-start(f32[1,64,256]{2,1,0:T(8,128)} %param.20) | copy-start | bytes 196612
  47.4 7.8 %all-to-all-start.1 = ((f32[2,1,64,256]{3,2,1,0:T(8,128)}), f32[2,1,64,256]{3,2,1,0:T(8,128)S(1)}, u32[]{:S(2)}, u32[]{:S(2)}) async-start(f32[2,1,64,256]{3,2,1,0:T(8,128)} %pad_maximum_fusion.1), calls=%async_computation.2 | async-start | bytes 262144 | tf_op jit(solution)/shard_map/all_to_all | solution.py:135
  50.8 31.1 %reduce-scatter.7.cloned.1.call-start = ((), (), s32[]{:S(2)}) async-start(), calls=%async_computation.9 | async-start | bytes 196608 | tf_op jit(solution)/shard_map/reduce_scatter | solution.py:146
  65.1 0.6 copy-start.6
  65.8 25.5 %copy-start.10 = (s32[1,2,512]{2,1,0:T(2,128)S(1)}, s32[1,2,512]{2,1,0:T(2,128)}, u32[]{:S(2)}) copy-start(s32[1,2,512]{2,1,0:T(2,128)} %param.28) | copy-start | bytes 12292
  65.8 33.4 %copy-start.5 = (s32[1,64,256]{2,1,0:T(8,128)S(1)}, s32[1,64,256]{2,1,0:T(8,128)}, u32[]{:S(2)}) copy-start(s32[1,64,256]{2,1,0:T(8,128)} %param.21) | copy-start | bytes 196612
  82.7 8.6 %collective-permute-start = (f32[1,64,256]{2,1,0:T(8,128)S(1)}, f32[1,64,256]{2,1,0:T(8,128)S(1)}, u32[]{:S(2)}, u32[]{:S(2)}) collective-permute-start(f32[1,64,256]{2,1,0:T(8,128)S(1)} %sub.153), channel_id=1, source_target_pairs={{1,0},{2,1},{3,2},{4,3},{5,4},{6,5},{7,6},{8,7},{9,8},{10,9},{11,1... | collective-permute-start | bytes 196616 | tf_op jit(solution)/shard_map/ppermute | solution.py:26
  89.4 9.8 %collective-permute-start.1 = (f32[1,64,256]{2,1,0:T(8,128)S(1)}, f32[1,64,256]{2,1,0:T(8,128)S(1)}, u32[]{:S(2)}, u32[]{:S(2)}) collective-permute-start(f32[1,64,256]{2,1,0:T(8,128)S(1)} %sub.153), channel_id=1, source_target_pairs={{0,1},{1,2},{2,3},{3,4},{4,5},{5,6},{6,7},{7,8},{8,9},{9,10},{10,1... | collective-permute-start | bytes 196616 | tf_op jit(solution)/shard_map/ppermute | solution.py:24
  100.0 7.8 %all-to-all-start.2 = ((f32[2,1,64,256]{3,2,1,0:T(8,128)}), f32[2,1,64,256]{3,2,1,0:T(8,128)S(1)}, u32[]{:S(2)}, u32[]{:S(2)}) async-start(f32[2,1,64,256]{3,2,1,0:T(8,128)} %pad_maximum_fusion.2), calls=%async_computation.4 | async-start | bytes 262144 | tf_op jit(solution)/shard_map/all_to_all | solution.py:135
  103.3 24.1 %reduce-scatter.9.cloned.1.call-start = ((), (), s32[]{:S(2)}) async-start(), calls=%async_computation.10 | async-start | bytes 196608 | tf_op jit(solution)/shard_map/reduce_scatter | solution.py:146
  117.7 0.6 copy-start.7
  129.0 3.7 %copy-start.13 = (s32[1,2]{1,0:T(1,128)S(1)}, s32[1,2]{1,0:T(1,128)}, u32[]{:S(2)}) copy-start(s32[1,2]{1,0:T(1,128)} %param.29) | copy-start | bytes 28
  129.0 8.0 %all-to-all-start.3 = ((f32[2,1,64,256]{3,2,1,0:T(8,128)}), f32[2,1,64,256]{3,2,1,0:T(8,128)S(1)}, u32[]{:S(2)}, u32[]{:S(2)}) async-start(f32[2,1,64,256]{3,2,1,0:T(8,128)} %pad_maximum_fusion.3), calls=%async_computation.6 | async-start | bytes 262144 | tf_op jit(solution)/shard_map/all_to_all | solution.py:135
  132.5 31.1 %reduce-scatter.11.cloned.1.call-start = ((), (), s32[]{:S(2)}) async-start(), calls=%async_computation.11 | async-start | bytes 196608 | tf_op jit(solution)/shard_map/reduce_scatter | solution.py:146
  146.9 0.6 copy-start.8
  147.5 6.2 %copy-start.1 = (f32[4096]{0:T(1024)}, f32[4096]{0:T(1024)S(1)}, u32[]{:S(2)}) copy-start(f32[4096]{0:T(1024)S(1)} %fusion.130) | copy-start | bytes 49156
  153.8 19.2 %collective-permute-start.5 = (f32[2,512]{1,0:T(2,128)S(1)}, f32[2,512]{1,0:T(2,128)S(1)}, u32[]{:S(2)}, u32[]{:S(2)}) collective-permute-start(f32[2,512]{1,0:T(2,128)S(1)} %get-tuple-element.809), channel_id=1, source_target_pairs={{2,0},{4,2},{6,4},{8,6},{10,8},{12,10},{14,12},{16,14},{18,16},{20... | collective-permute-start | bytes 12296 | tf_op jit(solution)/shard_map/ppermute | solution.py:36
  159.4 13.6 %collective-permute-start.4 = (f32[2,512]{1,0:T(2,128)S(1)}, f32[2,512]{1,0:T(2,128)S(1)}, u32[]{:S(2)}, u32[]{:S(2)}) collective-permute-start(f32[2,512]{1,0:T(2,128)S(1)} %get-tuple-element.808), channel_id=1, source_target_pairs={{0,2},{2,4},{4,6},{6,8},{8,10},{10,12},{12,14},{14,16},{16,18},{18... | collective-permute-start | bytes 12296 | tf_op jit(solution)/shard_map/ppermute | solution.py:36
  164.5 9.2 %collective-permute-start.2 = (f32[1,64,256]{2,1,0:T(8,128)S(1)}, f32[1,64,256]{2,1,0:T(8,128)S(1)}, u32[]{:S(2)}, u32[]{:S(2)}) collective-permute-start(f32[1,64,256]{2,1,0:T(8,128)S(1)} %sub.161), channel_id=1, source_target_pairs={{1,0},{2,1},{3,2},{4,3},{5,4},{6,5},{7,6},{8,7},{9,8},{10,9},{11,1... | collective-permute-start | bytes 196616 | tf_op jit(solution)/shard_map/ppermute | solution.py:26
  171.1 9.8 %collective-permute-start.3 = (f32[1,64,256]{2,1,0:T(8,128)S(1)}, f32[1,64,256]{2,1,0:T(8,128)S(1)}, u32[]{:S(2)}, u32[]{:S(2)}) collective-permute-start(f32[1,64,256]{2,1,0:T(8,128)S(1)} %sub.161), channel_id=1, source_target_pairs={{0,1},{1,2},{2,3},{3,4},{4,5},{5,6},{6,7},{7,8},{8,9},{9,10},{10,1... | collective-permute-start | bytes 196616 | tf_op jit(solution)/shard_map/ppermute | solution.py:24
Sparse Core Ops, SparseCore 0:
  27.6 18.2 reduce-scatter.4
  65.9 15.8 reduce-scatter.6
  118.5 8.9 reduce-scatter.8
  147.7 15.9 reduce-scatter.10
